TPU v7x, 256 devices: a whole 4x4x8 slice. The times are simulated.
256 devices in a mesh: rows: 32 (over z, x), feat: 8 (over y, core).
Axes of the slice: x: 4, y: 4, z: 8, core: 2. Of those that a mesh axis runs over, the one named last changes fastest.
Arguments:
- points: float32 [8, 131072], P(None, 'rows'), may hold values from -4 to 4
- freq_index: int32 [8, 16384], P(None, 'feat'), may hold values from -12 to 12
- log_density: float32 [16384], P('feat'), may hold values from -3 to 2.7
- targets: float32 [131072], P('rows'), may hold values from -16 to 16
- probes: int32 [31, 131072], P(None, 'rows'), may hold values 0 or 1
Outputs:
- solution: float32 [32, 131072], P(None, 'rows')
- residual: float32 [32, 131072], P(None, 'rows')
All inputs are finite; a program needn't handle non-finite values. No bound on the sum of `probes` on one device may be relied on, other than what follows from the above.
Results may differ from a plain program's by a relative error of at most 0.0025.
Values may be sent and summed in bfloat16 or wider, within the bound.
A program may use at most 128 MiB of HBM per device.

v0:
```python
import math

import jax
import jax.numpy as jnp
from jax import lax
from jax.sharding import PartitionSpec as P

FREQS = 16384
ITERS = 2


frequency_step = 0.25
noise_level = 1.0


def build_features(points, frequency, amplitude, block_rows):
    rows_here = points.shape[1]
    blocks = rows_here // block_rows
    feature_width = 2 * frequency.shape[1]

    def fill(block_index, table):
        first_row = (block_index * block_rows).astype(jnp.int32)
        point_block = lax.dynamic_slice_in_dim(points, first_row, block_rows, 1)
        phases = jnp.dot(
            point_block.T,
            frequency,
            precision=lax.Precision.HIGHEST,
            preferred_element_type=jnp.float32,
        )
        block = jnp.concatenate(
            [amplitude * jnp.cos(phases), amplitude * jnp.sin(phases)], axis=1
        ).astype(jnp.bfloat16)
        return lax.dynamic_update_slice_in_dim(table, block, first_row, 0)

    initial = jnp.zeros((rows_here, feature_width), jnp.bfloat16)
    return lax.fori_loop(0, blocks, fill, initial)


def squared_norm(values):
    return lax.psum(jnp.sum(values * values, axis=1), "rows")


def local(points, freq_index, log_density, targets, probes):
    rows_here = points.shape[1]
    block_rows = math.gcd(rows_here, 512)
    frequency = frequency_step * freq_index.astype(jnp.float32)
    amplitude = jnp.exp(0.5 * log_density) / math.sqrt(FREQS)
    features = build_features(points, frequency, amplitude, block_rows)
    right_sides = jnp.concatenate([targets[None, :], (2 * probes - 1).astype(jnp.float32)], axis=0)
    solution = jnp.zeros_like(right_sides)
    residual = right_sides
    direction = right_sides
    residual_energy = squared_norm(right_sides)
    for iteration in range(ITERS):
        direction_bf = direction.astype(jnp.bfloat16)
        partial_coeffs = jnp.dot(direction_bf, features, preferred_element_type=jnp.float32)
        coeff_bf = lax.psum(partial_coeffs, "rows").astype(jnp.bfloat16)
        coeff_bf = lax.optimization_barrier(coeff_bf)
        partial_images = lax.dot_general(
            coeff_bf, features, (((1,), (1,)), ((), ())), preferred_element_type=jnp.float32
        )
        coeff_wide = coeff_bf.astype(jnp.float32)
        energy_part = jnp.sum(coeff_wide * coeff_wide, axis=1)
        images = lax.psum(partial_images, "feat")
        feature_energy = lax.psum(energy_part, "feat")
        direction_energy = lax.psum(jnp.sum(direction * direction, axis=1), "rows")
        curvature = feature_energy + noise_level * direction_energy
        step_size = residual_energy / curvature
        solution = solution + step_size[:, None] * direction
        residual = residual - step_size[:, None] * (images + noise_level * direction)
        if iteration + 1 < ITERS:
            energy_next = squared_norm(residual)
            mixing = energy_next / residual_energy
            direction = residual + mixing[:, None] * direction
            residual_energy = energy_next
    return (solution, residual)


def solution(mesh):
    in_specs = (P(None, "rows"), P(None, "feat"), P("feat"), P("rows"), P(None, "rows"))
    out_specs = (P(None, "rows"), P(None, "rows"))
    return jax.shard_map(local, mesh=mesh, in_specs=in_specs, out_specs=out_specs, check_vma=False)
```

profile of v0, /device:TPU:1, one launch (start us, length us, event | category | flops | bytes accessed | tf_op | source)
XLA Modules:
  0.0 763.1 jit_solution(17343094420450126333)
XLA Ops:
  7.9 0.8 convert_multiply_fusion
  8.8 11.0 %broadcast_in_dim.9 = bf16[4096,4096]{1,0:T(8,128)(2,1)} broadcast(bf16[]{:T(256)} %constant.42.clone.1), dimensions={} | broadcast | bytes 33554432 | tf_op jit(solution)/shard_map/broadcast_in_dim | solution.py:35
  19.7 182.7 %while.13 = (s32[]{:T(128)}, bf16[4096,4096]{1,0:T(8,128)(2,1)}, f32[2048]{0:T(1024)S(1)}, f32[8,4096]{1,0:T(8,128)}, f32[8,2048]{1,0:T(8,128)S(1)}, /*index=5*/s32[]{:T(128)}, s32[]{:T(128)}, s32[]{:T(128)}, s32[]{:T(128)}) while((s32[]{:T(128)}, bf16[4096,4096]{1,0:T(8,128)(2,1)}, f32[2048]{0:T(1024)S(1)}, f32[8,4096]{1,0:T(8,128)}, ...), condition=%wide.region_3.0_spmd, body=%wide.region_2.0_spmd.sunk | while | flops 113246216 | bytes 12673179 | solution.py:36
  19.7 20.4 %multiply_convert_fusion.3 = (bf16[512,2048]{1,0:T(8,128)(2,1)S(1)}, bf16[512,2048]{1,0:T(8,128)(2,1)S(1)}) fusion(f32[2048]{0:T(1024)S(1)} %get-tuple-element.170, f32[8,2048]{1,0:T(8,128)S(1)} %get-tuple-element.172, f32[8,4096]{1,0:T(8,128)} %get-tuple-element.171, s32[]{:T(128)S(6)} %select_n.9), kind=kOutput, calls=%fused_computation.2.clone.1 | convolution fusion | flops 104857600 | bytes 4284420 | tf_op jit(solution)/shard_map/while/body/eval_jaxpr/dot_general | solution.py:24
  40.2 2.4 maximum_dynamic-update-slice_fusion.2
  42.6 20.4 %multiply_convert_fusion.3 = (bf16[512,2048]{1,0:T(8,128)(2,1)S(1)}, bf16[512,2048]{1,0:T(8,128)(2,1)S(1)}) fusion(f32[2048]{0:T(1024)S(1)} %get-tuple-element.170, f32[8,2048]{1,0:T(8,128)S(1)} %get-tuple-element.172, f32[8,4096]{1,0:T(8,128)} %get-tuple-element.171, s32[]{:T(128)S(6)} %select_n.9), kind=kOutput, calls=%fused_computation.2.clone.1 | convolution fusion | flops 104857600 | bytes 4284420 | tf_op jit(solution)/shard_map/while/body/eval_jaxpr/dot_general | solution.py:24
  63.0 2.5 maximum_dynamic-update-slice_fusion.2
  65.4 20.4 %multiply_convert_fusion.3 = (bf16[512,2048]{1,0:T(8,128)(2,1)S(1)}, bf16[512,2048]{1,0:T(8,128)(2,1)S(1)}) fusion(f32[2048]{0:T(1024)S(1)} %get-tuple-element.170, f32[8,2048]{1,0:T(8,128)S(1)} %get-tuple-element.172, f32[8,4096]{1,0:T(8,128)} %get-tuple-element.171, s32[]{:T(128)S(6)} %select_n.9), kind=kOutput, calls=%fused_computation.2.clone.1 | convolution fusion | flops 104857600 | bytes 4284420 | tf_op jit(solution)/shard_map/while/body/eval_jaxpr/dot_general | solution.py:24
  85.8 2.5 maximum_dynamic-update-slice_fusion.2
  88.3 20.4 %multiply_convert_fusion.3 = (bf16[512,2048]{1,0:T(8,128)(2,1)S(1)}, bf16[512,2048]{1,0:T(8,128)(2,1)S(1)}) fusion(f32[2048]{0:T(1024)S(1)} %get-tuple-element.170, f32[8,2048]{1,0:T(8,128)S(1)} %get-tuple-element.172, f32[8,4096]{1,0:T(8,128)} %get-tuple-element.171, s32[]{:T(128)S(6)} %select_n.9), kind=kOutput, calls=%fused_computation.2.clone.1 | convolution fusion | flops 104857600 | bytes 4284420 | tf_op jit(solution)/shard_map/while/body/eval_jaxpr/dot_general | solution.py:24
  108.7 2.5 maximum_dynamic-update-slice_fusion.2
  111.1 20.4 %multiply_convert_fusion.3 = (bf16[512,2048]{1,0:T(8,128)(2,1)S(1)}, bf16[512,2048]{1,0:T(8,128)(2,1)S(1)}) fusion(f32[2048]{0:T(1024)S(1)} %get-tuple-element.170, f32[8,2048]{1,0:T(8,128)S(1)} %get-tuple-element.172, f32[8,4096]{1,0:T(8,128)} %get-tuple-element.171, s32[]{:T(128)S(6)} %select_n.9), kind=kOutput, calls=%fused_computation.2.clone.1 | convolution fusion | flops 104857600 | bytes 4284420 | tf_op jit(solution)/shard_map/while/body/eval_jaxpr/dot_general | solution.py:24
  131.5 2.4 maximum_dynamic-update-slice_fusion.2
  133.9 20.4 %multiply_convert_fusion.3 = (bf16[512,2048]{1,0:T(8,128)(2,1)S(1)}, bf16[512,2048]{1,0:T(8,128)(2,1)S(1)}) fusion(f32[2048]{0:T(1024)S(1)} %get-tuple-element.170, f32[8,2048]{1,0:T(8,128)S(1)} %get-tuple-element.172, f32[8,4096]{1,0:T(8,128)} %get-tuple-element.171, s32[]{:T(128)S(6)} %select_n.9), kind=kOutput, calls=%fused_computation.2.clone.1 | convolution fusion | flops 104857600 | bytes 4284420 | tf_op jit(solution)/shard_map/while/body/eval_jaxpr/dot_general | solution.py:24
  154.3 2.5 maximum_dynamic-update-slice_fusion.2
  156.8 20.4 %multiply_convert_fusion.3 = (bf16[512,2048]{1,0:T(8,128)(2,1)S(1)}, bf16[512,2048]{1,0:T(8,128)(2,1)S(1)}) fusion(f32[2048]{0:T(1024)S(1)} %get-tuple-element.170, f32[8,2048]{1,0:T(8,128)S(1)} %get-tuple-element.172, f32[8,4096]{1,0:T(8,128)} %get-tuple-element.171, s32[]{:T(128)S(6)} %select_n.9), kind=kOutput, calls=%fused_computation.2.clone.1 | convolution fusion | flops 104857600 | bytes 4284420 | tf_op jit(solution)/shard_map/while/body/eval_jaxpr/dot_general | solution.py:24
  177.2 2.5 maximum_dynamic-update-slice_fusion.2
  179.6 20.4 %multiply_convert_fusion.3 = (bf16[512,2048]{1,0:T(8,128)(2,1)S(1)}, bf16[512,2048]{1,0:T(8,128)(2,1)S(1)}) fusion(f32[2048]{0:T(1024)S(1)} %get-tuple-element.170, f32[8,2048]{1,0:T(8,128)S(1)} %get-tuple-element.172, f32[8,4096]{1,0:T(8,128)} %get-tuple-element.171, s32[]{:T(128)S(6)} %select_n.9), kind=kOutput, calls=%fused_computation.2.clone.1 | convolution fusion | flops 104857600 | bytes 4284420 | tf_op jit(solution)/shard_map/while/body/eval_jaxpr/dot_general | solution.py:24
  200.0 2.4 maximum_dynamic-update-slice_fusion.2
  202.7 13.5 %fusion.5 = f32[32,4096]{1,0:T(8,128)S(1)} fusion(bf16[4096,4096]{1,0:T(8,128)(2,1)} %get-tuple-element.96, f32[31,4096]{1,0:T(8,128)S(1)} %add_convert_fusion, f32[1,4096]{1,0:T(1,128)S(1)} %bitcast.11), kind=kOutput, calls=%fused_computation.19 | convolution fusion | flops 1074266112 | bytes 34603008 | tf_op jit(solution)/shard_map/dot_general | solution.py:56
  216.3 125.5 %all-reduce.10 = (bf16[32,4096]{1,0:T(8,128)(2,1)S(1)}, f32[32]{0:T(128)S(1)}) all-reduce(f32[32,4096]{1,0:T(8,128)S(1)} %fusion.5, f32[32]{0:T(128)S(1)} %multiply_reduce_fusion.4), channel_id=1, replica_groups=mesh['rows'=32,'feat'=8] {'rows'}, use_global_device_ids=true, to_apply=%region_4.0 | all-reduce | flops 131104 | bytes 786688 | tf_op jit(solution)/shard_map/psum | solution.py:57
  341.8 16.0 %fusion.8 = f32[32,4096]{1,0:T(8,128)} fusion(bf16[32,4096]{1,0:T(8,128)(2,1)S(1)} %get-tuple-element.109, bf16[4096,4096]{1,0:T(8,128)(2,1)} %get-tuple-element.96), kind=kOutput, calls=%fused_computation.26 | convolution fusion | flops 1073741824 | bytes 34340864 | tf_op jit(solution)/shard_map/dot_general | solution.py:59
  358.0 39.9 %psum.68 = f32[32]{0:T(128)S(1)} all-reduce(f32[32]{0:T(128)S(1)} %multiply_reduce_fusion.3), channel_id=1, replica_groups=mesh['rows'=32,'feat'=8] {'feat'}, use_global_device_ids=true, to_apply=%region_6.0 | all-reduce | flops 32 | bytes 256 | tf_op jit(solution)/shard_map/psum | solution.py:65
  398.0 45.9 %all-reduce.7.cloned.1.call-done = f32[32,4096]{1,0:T(8,128)} async-done(((f32[32,4096]{1,0:T(8,128)}), f32[32,4096]{1,0:T(8,128)}) %all-reduce.7.cloned.1.call-update) | async-done | bytes 524304 | tf_op jit(solution)/shard_map/psum | solution.py:64
  443.9 1.4 multiply_reduce_fusion.2
  445.2 61.0 %psum.70 = f32[32]{0:T(128)S(1)} all-reduce(f32[32]{0:T(128)S(1)} %multiply_reduce_fusion.2), channel_id=1, replica_groups=mesh['rows'=32,'feat'=8] {'rows'}, use_global_device_ids=true, to_apply=%region_9.0 | all-reduce | flops 32 | bytes 256 | tf_op jit(solution)/shard_map/psum | solution.py:40
  506.3 13.8 %fusion.3 = f32[32,4096]{1,0:T(8,128)S(1)} fusion(bf16[4096,4096]{1,0:T(8,128)(2,1)} %get-tuple-element.96, f32[32]{0:T(128)S(1)} %div.18, f32[31,4096]{1,0:T(8,128)S(1)} %add_convert_fusion, f32[1,4096]{1,0:T(1,128)S(1)} %bitcast.13, f32[32,4096]{1,0:T(8,128)} %all-reduce.7.cloned.1.call-done, f32[32]{0:T(128)S(1)} %add_divide_fusion), kind=kOutput, calls=%fused_computation.17 | convolution fusion | flops 1074659328 | bytes 35127552 | tf_op jit(solution)/shard_map/dot_general | solution.py:56
  520.3 116.2 %all-reduce.11 = (bf16[32,4096]{1,0:T(8,128)(2,1)S(1)}, f32[32]{0:T(128)S(1)}) all-reduce(f32[32,4096]{1,0:T(8,128)S(1)} %fusion.3, f32[32]{0:T(128)S(1)} %multiply_reduce_fusion), channel_id=1, replica_groups=mesh['rows'=32,'feat'=8] {'rows'}, use_global_device_ids=true, to_apply=%region_10.0 | all-reduce | flops 131104 | bytes 786688 | tf_op jit(solution)/shard_map/psum | solution.py:57
  636.5 16.0 %fusion.9 = f32[32,4096]{1,0:T(8,128)} fusion(bf16[32,4096]{1,0:T(8,128)(2,1)S(1)} %get-tuple-element.107, bf16[4096,4096]{1,0:T(8,128)(2,1)} %get-tuple-element.96), kind=kOutput, calls=%fused_computation.27 | convolution fusion | flops 1073741824 | bytes 34340864 | tf_op jit(solution)/shard_map/dot_general | solution.py:59
  652.7 56.2 %psum.72 = f32[32]{0:T(128)S(1)} all-reduce(f32[32]{0:T(128)S(1)} %multiply_reduce_fusion.1), channel_id=1, replica_groups=mesh['rows'=32,'feat'=8] {'feat'}, use_global_device_ids=true, to_apply=%region_12.0 | all-reduce | flops 32 | bytes 256 | tf_op jit(solution)/shard_map/psum | solution.py:65
  708.9 45.0 %all-reduce.9.cloned.1.call-done = f32[32,4096]{1,0:T(8,128)} async-done(((f32[32,4096]{1,0:T(8,128)}), f32[32,4096]{1,0:T(8,128)}) %all-reduce.9.cloned.1.call-update) | async-done | bytes 524304 | tf_op jit(solution)/shard_map/psum | solution.py:64
  754.0 2.3 multiply_subtract_fusion
  (19 shorter events, 1.8 us)
Async XLA Ops:
  7.2 436.7 %all-reduce.7.cloned.1.call-start = ((), (), s32[]{:S(2)}) async-start(), calls=%async_computation | async-start | bytes 1048576 | tf_op jit(solution)/shard_map/psum | solution.py:64
  19.7 182.7 %copy-start.2 = (s32[31,4096]{1,0:T(8,128)S(1)}, s32[31,4096]{1,0:T(8,128)}, u32[]{:S(2)}) copy-start(s32[31,4096]{1,0:T(8,128)} %param.11) | copy-start | bytes 1523716
  19.7 182.8 %copy-start.1 = (f32[4096]{0:T(1024)S(1)}, f32[4096]{0:T(1024)}, u32[]{:S(2)}) copy-start(f32[4096]{0:T(1024)} %param.10) | copy-start | bytes 49156
  357.8 396.1 %all-reduce.9.cloned.1.call-start = ((), (), s32[]{:S(2)}) async-start(), calls=%async_computation.1 | async-start | bytes 1048576 | tf_op jit(solution)/shard_map/psum | solution.py:64
  443.8 76.2 %copy-start = (f32[32,4096]{1,0:T(8,128)S(1)}, f32[32,4096]{1,0:T(8,128)}, u32[]{:S(2)}) copy-start(f32[32,4096]{1,0:T(8,128)} %all-reduce.7.cloned.1.call-done) | copy-start | bytes 1572868
Sparse Core Ops, SparseCore 0:
  357.9 85.8 all-reduce.6
  652.7 101.2 all-reduce.8
where the time goes:
time: 765 us; the launch traced here: 763 us
  blocking collectives  399 us (52%)
  matrix products  222 us (29%)
  waiting for transfers between devices  90.9 us (12%)
  other arithmetic  25.8 us (3%)
  between operations  14.1 us (2%)
  local copies, waits for them, and re-layouts  11 us (1%)
    psum x2, blocking collectives, local(): coeff_bf = lax.psum(partial_coeffs, 'rows').astype(jnp.bfloat16)  242 us
    dot_general x8, matrix products, fill(): jnp.dot(point_block.T, frequency, precision=lax.Precision.HIGHEST, prefer...  163 us
    psum x2, blocking collectives, local(): feature_energy = lax.psum(energy_part, 'feat')  96.1 us
    psum x2, waiting for transfers between devices, local(): images = lax.psum(partial_images, 'feat')  90.9 us
    psum x1, blocking collectives, squared_norm(): return lax.psum(jnp.sum(values * values, axis=1), 'rows')  61 us
    dot_general x2, matrix products, local(): lax.dot_general(coeff_bf, features, (((1,), (1,)), ((), ())), preferred_e...  32 us
    dot_general x2, matrix products, local(): jnp.dot(direction_bf, features, preferred_element_type=jnp.float32)  27.3 us
    dynamic_update_slice x8, other arithmetic, fill(): return lax.dynamic_update_slice_in_dim(table, block, first_row, 0)  19.7 us
  transfers between devices with their start and end apart: 2, of which 2 were waited for; matrix products, arithmetic and copies ran while one was open for 0% of the time, Pallas kernels for 0%

commit v1 on v0

v1 whole, which is shorter than its diff:
```python
import functools
import math

import jax
import jax.numpy as jnp
from jax import lax
from jax.experimental import pallas as pl
from jax.experimental.pallas import tpu as pltpu
from jax.sharding import PartitionSpec as P

FREQS = 16384
LANES = 128
TURN = 0.25 / (2.0 * math.pi)
SIN_TERMS = (4.44286798219978, -7.307445410802044, 3.594802081647382, -0.7844035671777289)
COS_TERMS = (
    1.4142134965673496,
    -6.9788509883336225,
    5.739461171609176,
    -1.8835629899096435,
    0.310698192272404,
)
F32 = jnp.float32
BF16 = jnp.bfloat16
MESH = pl.DeviceIdType.MESH


def scaled_trig(turns, amplitude):
    r = turns - jnp.round(turns)
    u = r * r
    half_sin = SIN_TERMS[-1]
    for term in SIN_TERMS[-2::-1]:
        half_sin = half_sin * u + term
    half_sin = half_sin * r
    half_cos = COS_TERMS[-1]
    for term in COS_TERMS[-2::-1]:
        half_cos = half_cos * u + term
    scaled = amplitude * half_sin
    return amplitude - scaled * half_sin, scaled * half_cos


def three_way(value):
    high = value.astype(BF16).astype(F32)
    middle = (value - high).astype(BF16).astype(F32)
    return high, middle, value - high - middle


def spread(value, axis, shape):
    high, middle, low = three_way(value)
    place = lax.broadcasted_iota(jnp.int32, shape, axis)
    high, middle, low = (jnp.broadcast_to(part, shape) for part in (high, middle, low))
    zero = jnp.zeros(shape, F32)
    return jnp.where(
        place == 0, high, jnp.where(place == 1, middle, jnp.where(place == 2, low, zero))
    )


def lane_fold(value):
    total = value[:, :LANES]
    for start in range(LANES, value.shape[1], LANES):
        total = total + value[:, start : start + LANES]
    return total


def rows_to_lanes(parts):
    stacked = jnp.concatenate(parts, axis=0)
    rest = LANES - stacked.shape[0]
    stacked = jnp.concatenate([stacked, jnp.zeros((rest, LANES), F32)], axis=0)
    return jnp.sum(stacked.T, axis=0, keepdims=True)


def lanes_to_rows(row, offset, count):
    shape = (count, LANES)
    here = lax.broadcasted_iota(jnp.int32, shape, 0) + offset
    lane = lax.broadcasted_iota(jnp.int32, shape, 1)
    picked = jnp.where(here == lane, jnp.broadcast_to(row, shape), jnp.zeros(shape, F32))
    return jnp.sum(picked, axis=1, keepdims=True)


def kernel(
    sizes, points, freq, density, targets, probes, x_out, r_out,
    table, turns_t, rhs, rhs_bf,
    c_part, c_send, c_recv, c_own, c_all, s_send, s_recv, d_all,
    i_part, i_send, i_recv, i_all, j_send, j_recv, j_all,
    a_src, b_src, c_src, d_src, send_sem, recv_sem,
):
    rows, feats = sizes
    me_r = lax.axis_index("rows")
    me_f = lax.axis_index("feat")
    here = points.shape[1]
    width = freq.shape[1]
    sides = rhs.shape[0]
    share = here // feats
    batch_r = min(512, here)
    batch_f = min(256, width)

    barrier = pltpu.get_barrier_semaphore()

    def greet_row(step, carry):
        pl.semaphore_signal(
            barrier, inc=1, device_id=(lax.rem(me_r + step, rows), me_f), device_id_type=MESH
        )
        return carry

    def greet_feat(step, carry):
        pl.semaphore_signal(
            barrier, inc=1, device_id=(me_r, lax.rem(me_f + step, feats)), device_id_type=MESH
        )
        return carry

    lax.fori_loop(1, rows, greet_row, 0)
    lax.fori_loop(1, feats, greet_feat, 0)

    def to_row(phase, src, dst, step):
        return pltpu.make_async_remote_copy(
            src_ref=src, dst_ref=dst, send_sem=send_sem.at[phase], recv_sem=recv_sem.at[phase],
            device_id=(lax.rem(me_r + step, rows), me_f), device_id_type=MESH,
        )

    def to_feat(phase, src, dst, step):
        return pltpu.make_async_remote_copy(
            src_ref=src, dst_ref=dst, send_sem=send_sem.at[phase], recv_sem=recv_sem.at[phase],
            device_id=(me_r, lax.rem(me_f + step, feats)), device_id_type=MESH,
        )

    def await_bytes(sem, ref):
        pltpu.make_async_copy(ref, ref, sem).wait()

    rhs[0:1, :] = targets[...]
    rhs[1:sides, :] = (2 * probes[...] - 1).astype(F32)
    right = rhs[...]
    rhs_bf[...] = right.astype(BF16)
    scaled = points[...] * TURN
    high, middle, low = three_way(scaled)
    stacked = jnp.concatenate([high, middle, low, jnp.zeros_like(high)], axis=0)
    turns_t[...] = stacked.T.astype(BF16)
    tail = spread(rows_to_lanes([lane_fold(right * right)]), 0, (16, LANES)).astype(BF16)

    def set_tail(buffer, tail):
        def put(chunk, carry):
            buffer[chunk, sides : sides + 16, :] = tail
            return carry

        lax.fori_loop(0, rows, put, 0)

    set_tail(c_send, tail)
    pl.semaphore_wait(barrier, rows + feats - 2)

    def ship(phase, buffer, landing, chunk, value, keep):
        buffer[chunk, 0:sides, :] = value.astype(BF16)
        step = lax.rem(chunk + rows - me_r, rows)

        @pl.when(chunk == me_r)
        def _():
            keep[...] = value

        @pl.when(chunk != me_r)
        def _():
            to_row(phase, buffer.at[chunk], landing.at[step - 1], step).start()

    blocks_f = width // batch_f
    per_block = batch_f // LANES
    half = rows // 2
    own_block = lax.rem(me_r, half) // per_block

    def make_block(index, carry):
        block = lax.rem(index + own_block + 1, blocks_f)
        at = pl.multiple_of(block * batch_f, batch_f)
        whole = freq[:, pl.ds(at, batch_f)].astype(F32)
        whole = jnp.concatenate([whole, whole, whole, jnp.zeros_like(whole)], axis=0).astype(BF16)
        strength = jnp.exp(0.5 * density[:, pl.ds(at, batch_f)]) * (1.0 / math.sqrt(FREQS))

        def fill(step, carry):
            first = pl.multiple_of(step * batch_r, batch_r)
            turns = jnp.dot(
                turns_t[pl.ds(first, batch_r), :], whole, preferred_element_type=F32
            )
            cosine, sine = scaled_trig(turns, strength)
            table[pl.ds(first, batch_r), pl.ds(at, batch_f)] = cosine.astype(BF16)
            table[pl.ds(first, batch_r), pl.ds(width + at, batch_f)] = sine.astype(BF16)
            return carry

        lax.fori_loop(0, here // batch_r, fill, 0)
        for part in range(2):
            sums = jnp.dot(
                rhs_bf[...],
                table[:, pl.ds(part * width + at, batch_f)],
                preferred_element_type=F32,
            )
            for piece in range(per_block):
                chunk = part * half + block * per_block + piece
                ship(0, c_send, c_recv, chunk, sums[:, piece * LANES : (piece + 1) * LANES], c_part)
        return carry

    lax.fori_loop(0, blocks_f, make_block, 0)

    def collect_rows(phase, landing, buffer, own):
        await_bytes(recv_sem.at[phase], landing)

        def add(slot, carry):
            total, extra = carry
            total = total + landing[slot, 0:sides, :].astype(F32)
            return total, extra + landing[slot, sides : sides + 16, :].astype(F32)

        first = (own[...], buffer[0, sides : sides + 16, :].astype(F32))
        total, extra = lax.fori_loop(0, rows - 1, add, first)
        return total, jnp.sum(extra, axis=0, keepdims=True)

    def share_rows(phase, source, everyone, value):
        source[...] = value
        everyone[me_r] = value

        def send(step, carry):
            to_row(phase, source, everyone.at[me_r], step).start()
            return carry

        lax.fori_loop(1, rows, send, 0)
        await_bytes(recv_sem.at[phase], everyone.at[pl.ds(0, rows - 1)])

    total, extra = collect_rows(0, c_recv, c_send, c_part)
    energy = lanes_to_rows(extra, 0, sides)
    c_own[...] = total
    share_rows(1, a_src, c_all, total.astype(BF16))

    def spread_up(phase, everyone, buffer, landing, own):
        wide = everyone_cat(everyone).astype(F32)
        squares = jnp.sum(lane_fold(wide * wide), axis=1, keepdims=True)
        tail = jnp.where(
            lax.broadcasted_iota(jnp.int32, (sides, LANES), 1) == 0,
            jnp.broadcast_to(squares, (sides, LANES)),
            jnp.zeros((sides, LANES), F32),
        )

        def one(index, carry):
            step = index + 1
            target = lax.rem(me_f + step, feats)
            at = pl.multiple_of(target * share, share)
            images = lax.dot_general(
                everyone_cat(everyone), table[pl.ds(at, share), :],
                (((1,), (1,)), ((), ())), preferred_element_type=F32,
            )
            buffer[target, :, 0:share] = images
            buffer[target, :, share : share + LANES] = tail

            @pl.when(step < feats)
            def _():
                to_feat(phase, buffer.at[target], landing.at[step - 1], step).start()

            @pl.when(step == feats)
            def _():
                own[...] = images

            return carry

        lax.fori_loop(0, feats, one, 0)
        await_bytes(recv_sem.at[phase], landing)
        total = own[...]
        extra = tail
        for slot in range(feats - 1):
            total = total + landing[slot, :, 0:share]
            extra = extra + landing[slot, :, share : share + LANES]
        return total, jnp.sum(extra, axis=1, keepdims=True)

    def everyone_cat(everyone):
        return jnp.concatenate([everyone[chunk] for chunk in range(rows)], axis=1)

    def share_feats(phase, source, everyone, value):
        source[...] = value
        everyone[me_f] = value

        def send(step, carry):
            to_feat(phase, source, everyone.at[me_f], step).start()
            return carry

        lax.fori_loop(1, feats, send, 0)
        await_bytes(recv_sem.at[phase], everyone.at[pl.ds(0, feats - 1)])

    total, squares = spread_up(2, c_all, i_send, i_recv, i_part)
    alpha0 = energy / (squares + energy)
    share_feats(3, b_src, i_all, total)

    def images_of(everyone):
        return jnp.concatenate([everyone[part] for part in range(feats)], axis=1)

    images = images_of(i_all)
    rhs_bf[...] = images.astype(BF16)
    residual = (1.0 - alpha0) * rhs[...] - alpha0 * images
    cross = lane_fold(residual * rhs[...])
    tail = spread(rows_to_lanes([lane_fold(residual * residual), cross]), 0, (16, LANES))
    set_tail(s_send, tail.astype(BF16))

    group = min(4, rows)
    blocks_d = rows // group
    own_group = me_r // group

    def project(index, carry):
        block = lax.rem(index + own_group + 1, blocks_d)
        at = pl.multiple_of(block * (group * LANES), group * LANES)
        sums = jnp.dot(
            rhs_bf[...], table[:, pl.ds(at, group * LANES)], preferred_element_type=F32
        )
        for piece in range(group):
            chunk = block * group + piece
            ship(4, s_send, s_recv, chunk, sums[:, piece * LANES : (piece + 1) * LANES], c_part)
        return carry

    lax.fori_loop(0, blocks_d, project, 0)
    total, extra = collect_rows(4, s_recv, s_send, c_part)
    energy_next = lanes_to_rows(extra, 0, sides)
    cross = lanes_to_rows(extra, sides, sides)
    beta = energy_next / energy
    total = (1.0 - alpha0 + beta) * c_own[...] - alpha0 * total
    share_rows(5, c_src, d_all, total.astype(BF16))

    total, squares = spread_up(6, d_all, j_send, j_recv, i_part)
    direction_energy = energy_next + beta * (2.0 * cross + beta * energy)
    alpha1 = energy_next / (squares + direction_energy)
    share_feats(7, d_src, j_all, total)

    right = rhs[...]
    first_images = images_of(i_all)
    second_images = images_of(j_all)
    residual = (1.0 - alpha0) * right - alpha0 * first_images
    direction = residual + beta * right
    x_out[...] = alpha0 * right + alpha1 * direction
    r_out[...] = residual - alpha1 * (second_images + direction)

    for phase, ref in (
        (0, c_send.at[pl.ds(0, rows - 1)]), (1, c_all.at[pl.ds(0, rows - 1)]),
        (2, i_send.at[pl.ds(0, feats - 1)]), (3, i_all.at[pl.ds(0, feats - 1)]),
        (4, s_send.at[pl.ds(0, rows - 1)]), (5, d_all.at[pl.ds(0, rows - 1)]),
        (6, j_send.at[pl.ds(0, feats - 1)]), (7, j_all.at[pl.ds(0, feats - 1)]),
    ):
        await_bytes(send_sem.at[phase], ref)


def local(sizes, points, freq_index, log_density, targets, probes):
    rows, feats = sizes
    here = points.shape[1]
    width = freq_index.shape[1]
    sides = probes.shape[0] + 1
    share = here // feats
    vmem = pl.BlockSpec(memory_space=pltpu.VMEM)
    out = jax.ShapeDtypeStruct((sides, here), F32)
    block = (sides + 16, LANES)
    wide = (sides, share + LANES)
    scratch = [
        pltpu.VMEM((here, 2 * width), BF16),
        pltpu.VMEM((here, 32), BF16),
        pltpu.VMEM((sides, here), F32),
        pltpu.VMEM((sides, here), BF16),
        pltpu.VMEM((sides, LANES), F32),
        pltpu.VMEM((rows, *block), BF16),
        pltpu.VMEM((rows - 1, *block), BF16),
        pltpu.VMEM((sides, LANES), F32),
        pltpu.VMEM((rows, sides, LANES), BF16),
        pltpu.VMEM((rows, *block), BF16),
        pltpu.VMEM((rows - 1, *block), BF16),
        pltpu.VMEM((rows, sides, LANES), BF16),
        pltpu.VMEM((sides, share), F32),
        pltpu.VMEM((feats, *wide), F32),
        pltpu.VMEM((feats - 1, *wide), F32),
        pltpu.VMEM((feats, sides, share), F32),
        pltpu.VMEM((feats, *wide), F32),
        pltpu.VMEM((feats - 1, *wide), F32),
        pltpu.VMEM((feats, sides, share), F32),
        pltpu.VMEM((sides, LANES), BF16),
        pltpu.VMEM((sides, share), F32),
        pltpu.VMEM((sides, LANES), BF16),
        pltpu.VMEM((sides, share), F32),
        pltpu.SemaphoreType.DMA((8,)),
        pltpu.SemaphoreType.DMA((8,)),
    ]
    return pl.pallas_call(
        functools.partial(kernel, sizes),
        out_shape=(out, out),
        in_specs=[vmem] * 5,
        out_specs=(vmem, vmem),
        scratch_shapes=scratch,
        name="regress",
        compiler_params=pltpu.CompilerParams(
            collective_id=0, has_side_effects=True, vmem_limit_bytes=56 << 20
        ),
    )(points, freq_index, log_density.reshape(1, width), targets.reshape(1, here), probes)


def solution(mesh):
    sizes = (mesh.shape["rows"], mesh.shape["feat"])
    in_specs = (P(None, "rows"), P(None, "feat"), P("feat"), P("rows"), P(None, "rows"))
    out_specs = (P(None, "rows"), P(None, "rows"))
    return jax.shard_map(
        functools.partial(local, sizes),
        mesh=mesh, in_specs=in_specs, out_specs=out_specs, check_vma=False,
    )
```

time: 765 us -> 145 us (0.19)
  blocking collectives: 399 us -> 0 us
  matrix products: 222 us -> 0 us
  Pallas kernels: 0 us -> 141 us
  waiting for transfers between devices: 90.9 us -> 0 us
  other arithmetic: 25.8 us -> 0 us
  between operations: 14.1 us -> 0.65 us
  local copies, waits for them, and re-layouts: 11 us -> 2.72 us
    psum x5 -> x0, blocking collectives: 399 us -> none  [the longest x2 242 us: local(): coeff_bf = lax.psum(partial_coeffs, 'rows').astype(jnp.bfloat16)]
    dot_general x12 -> x0, matrix products: 222 us -> none  [the longest x8 163 us: fill(): jnp.dot(point_block.T, frequency, precision=lax.Precision.HIGHEST, prefer...]
    pallas_call x0 -> x1, Pallas kernels: none -> 141 us  [local(): pl.pallas_call(functools.partial(kernel, sizes), out_shape=(out, out), in...]
    psum x2 -> x0, waiting for transfers between devices: 90.9 us -> none  [local(): images = lax.psum(partial_images, 'feat')]
    dynamic_update_slice x8 -> x0, other arithmetic: 19.7 us -> none  [fill(): return lax.dynamic_update_slice_in_dim(table, block, first_row, 0)]
    broadcast_in_dim x1 -> x0, local copies, waits for them, and re-layouts: 11 us -> none  [build_features(): initial = jnp.zeros((rows_here, feature_width), jnp.bfloat16)]
  transfers between devices with their start and end apart: 2 -> 0, of which waited for: 2 -> 0; matrix products, arithmetic and copies ran while one was open for 0% -> 0% of each run, Pallas kernels for 0% -> 0%
where the time goes in v1:
time: 145 us
  Pallas kernels  141 us (97%)
  local copies, waits for them, and re-layouts  2.72 us (2%)
    pallas_call x1, Pallas kernels, local(): pl.pallas_call(functools.partial(kernel, sizes), out_shape=(out, out), in...  141 us

profile of v1, /device:TPU:1, one launch (start us, length us, event | category | flops | bytes accessed | tf_op | source)
XLA Modules:
  0.0 144.5 jit_solution(16569029561325241749)
XLA Ops:
  0.6 141.2 %regress.1 = (f32[32,4096]{1,0:T(8,128)}, f32[32,4096]{1,0:T(8,128)}) custom-call(f32[8,4096]{1,0:T(8,128)} %points.1, s32[8,2048]{1,0:T(8,128)} %freq.1, f32[1,2048]{1,0:T(1,128)} %bitcast.3, f32[1,4096]{1,0:T(1,128)} %bitcast.2, s32[31,4096]{1,0:T(8,128)} %probes.1), custom_call_target="tpu_custom_call" | custom-call | tf_op jit(solution)/shard_map/regress/pallas_call | solution.py:373
  141.8 0.0 copy-start
  141.8 1.9 %copy.9 = f32[32,4096]{1,0:T(8,128)} copy(f32[32,4096]{1,0:T(8,128)} %get-tuple-element.4) | data formatting | bytes 1048576
  143.7 0.0 copy-done
  143.7 0.8 copy.10
Async XLA Ops:
  141.8 1.9 %copy-start = (f32[32,4096]{1,0:T(8,128)S(1)}, f32[32,4096]{1,0:T(8,128)}, u32[]{:S(2)}) copy-start(f32[32,4096]{1,0:T(8,128)} %get-tuple-element.5) | copy-start | bytes 1572868

commit v2 on v1

v2 whole, which is shorter than its diff:
```python
import functools
import math

import jax
import jax.numpy as jnp
from jax import lax
from jax.experimental import pallas as pl
from jax.experimental.pallas import tpu as pltpu
from jax.sharding import PartitionSpec as P

FREQS = 16384
LANES = 128
TURN = 0.25 / (2.0 * math.pi)
SIN_TERMS = (4.44286798219978, -7.307445410802044, 3.594802081647382, -0.7844035671777289)
COS_TERMS = (1.414204080722155, -6.977642062283957, 5.715238417642065, -1.728348665863172)
F32 = jnp.float32
BF16 = jnp.bfloat16
MESH = pl.DeviceIdType.MESH


def scaled_trig(turns, amplitude):
    r = turns - jnp.round(turns)
    u = r * r
    half_sin = SIN_TERMS[-1]
    for term in SIN_TERMS[-2::-1]:
        half_sin = half_sin * u + term
    half_sin = half_sin * r
    half_cos = COS_TERMS[-1]
    for term in COS_TERMS[-2::-1]:
        half_cos = half_cos * u + term
    scaled = amplitude * half_sin
    return amplitude - scaled * half_sin, scaled * half_cos


def three_way(value):
    high = value.astype(BF16).astype(F32)
    middle = (value - high).astype(BF16).astype(F32)
    return high, middle, value - high - middle


def spread(value, axis, shape):
    high, middle, low = three_way(value)
    place = lax.broadcasted_iota(jnp.int32, shape, axis)
    high, middle, low = (jnp.broadcast_to(part, shape) for part in (high, middle, low))
    zero = jnp.zeros(shape, F32)
    return jnp.where(
        place == 0, high, jnp.where(place == 1, middle, jnp.where(place == 2, low, zero))
    )


def lane_fold(value):
    total = value[:, :LANES]
    for start in range(LANES, value.shape[1], LANES):
        total = total + value[:, start : start + LANES]
    return total


def rows_to_lanes(parts):
    stacked = jnp.concatenate(parts, axis=0)
    rest = LANES - stacked.shape[0]
    stacked = jnp.concatenate([stacked, jnp.zeros((rest, LANES), F32)], axis=0)
    return jnp.sum(stacked.T, axis=0, keepdims=True)


def lanes_to_rows(row, offset, count):
    shape = (count, LANES)
    here = lax.broadcasted_iota(jnp.int32, shape, 0) + offset
    lane = lax.broadcasted_iota(jnp.int32, shape, 1)
    picked = jnp.where(here == lane, jnp.broadcast_to(row, shape), jnp.zeros(shape, F32))
    return jnp.sum(picked, axis=1, keepdims=True)


def kernel(
    sizes, points, freq, density, targets, probes, x_out, r_out,
    table, turns_t, rhs, lhs, acc,
    c_part, c_send, c_recv, c_own, c_all, s_send, s_recv, d_all,
    i_part, i_own, i_send, i_recv, i_all, j_send, j_recv, j_all, g_all, h_all,
    a_src, b_src, c_src, d_src, e_src, f_src, send_sem, recv_sem, gather_sem,
):
    rows, feats = sizes
    me_r = lax.axis_index("rows")
    me_f = lax.axis_index("feat")
    here = points.shape[1]
    width = freq.shape[1]
    sides = rhs.shape[0]
    share = here // feats
    blocks = block_count(rows)
    members = rows // blocks
    span = width // blocks
    batch = min(1024, here)
    my_block = lax.rem(me_r, blocks)
    my_place = my_block * members + me_r // blocks

    barrier = pltpu.get_barrier_semaphore()

    def greet_row(step, carry):
        pl.semaphore_signal(
            barrier, inc=1, device_id=(lax.rem(me_r + step, rows), me_f), device_id_type=MESH
        )
        return carry

    def greet_feat(step, carry):
        pl.semaphore_signal(
            barrier, inc=1, device_id=(me_r, lax.rem(me_f + step, feats)), device_id_type=MESH
        )
        return carry

    lax.fori_loop(1, rows, greet_row, 0)
    lax.fori_loop(1, feats, greet_feat, 0)

    def to_row(phase, arrival, src, dst, step):
        return pltpu.make_async_remote_copy(
            src_ref=src, dst_ref=dst, send_sem=send_sem.at[phase], recv_sem=arrival,
            device_id=(lax.rem(me_r + step, rows), me_f), device_id_type=MESH,
        )

    def to_feat(phase, src, dst, step):
        return pltpu.make_async_remote_copy(
            src_ref=src, dst_ref=dst, send_sem=send_sem.at[phase], recv_sem=recv_sem.at[phase],
            device_id=(me_r, lax.rem(me_f + step, feats)), device_id_type=MESH,
        )

    def await_bytes(sem, ref):
        pltpu.make_async_copy(ref, ref, sem).wait()

    rhs[0:1, :] = targets[...]
    rhs[1:sides, :] = (2 * probes[...] - 1).astype(F32)
    right = rhs[...]
    lhs[...] = right.astype(BF16)
    high, middle, low = three_way(points[...] * TURN)
    stacked = jnp.concatenate([high, middle, low, jnp.zeros_like(high)], axis=0)
    turns_t[...] = stacked.T.astype(BF16)
    tail = spread(rows_to_lanes([lane_fold(right * right)]), 0, (16, LANES)).astype(BF16)

    def set_tail(buffer, tail):
        def put(chunk, carry):
            buffer[chunk, sides : sides + 16, :] = tail
            return carry

        lax.fori_loop(0, rows, put, 0)

    set_tail(c_send, tail)

    def make_block(block):
        at = block * span
        whole = freq[:, at : at + span].astype(F32)
        whole = jnp.concatenate([whole, whole, whole, jnp.zeros_like(whole)], axis=0).astype(BF16)
        strength = jnp.exp(0.5 * density[:, at : at + span]) * (1.0 / math.sqrt(FREQS))

        def fill(step, carry):
            first = pl.multiple_of(step * batch, batch)
            turns = jnp.dot(turns_t[pl.ds(first, batch), :], whole, preferred_element_type=F32)
            cosine, sine = scaled_trig(turns, strength)
            table[pl.ds(first, batch), 2 * at : 2 * at + span] = cosine.astype(BF16)
            table[pl.ds(first, batch), 2 * at + span : 2 * (at + span)] = sine.astype(BF16)
            return carry

        lax.fori_loop(0, here // batch, fill, 0)

    def project(block, buffer):
        for part in range(2):
            at = (2 * block + part) * span
            sums = jnp.dot(lhs[...], table[:, at : at + span], preferred_element_type=F32)
            for piece in range(span // LANES):
                member = part * (members // 2) + piece
                value = sums[:, piece * LANES : (piece + 1) * LANES]
                buffer[block * members + member, 0:sides, :] = value.astype(BF16)

                @pl.when(me_r == member * blocks + block)
                def _():
                    c_part[...] = value

    def ship(phase, block, buffer, landing):
        def send(member, carry):
            step = lax.rem(member * blocks + block + rows - me_r, rows)

            @pl.when(step != 0)
            def _():
                to_row(
                    phase, recv_sem.at[phase], buffer.at[block * members + member],
                    landing.at[step - 1], step,
                ).start()

            return carry

        lax.fori_loop(0, members, send, 0)

    def collect(phase, landing, buffer):
        await_bytes(recv_sem.at[phase], landing)

        def add(slot, carry):
            total, extra = carry
            total = total + landing[slot, 0:sides, :].astype(F32)
            return total, extra + landing[slot, sides : sides + 16, :].astype(F32)

        first = (c_part[...], buffer[0, sides : sides + 16, :].astype(F32))
        total, extra = lax.fori_loop(0, rows - 1, add, first)
        return total, jnp.sum(extra, axis=0, keepdims=True)

    def share_rows(phase, block, source, everyone, value):
        source[...] = value
        everyone[my_place] = value

        def send(step, carry):
            arrival = gather_sem.at[phase // 4, block]
            to_row(phase, arrival, source, everyone.at[my_place], step).start()
            return carry

        lax.fori_loop(1, rows, send, 0)

    def await_block(phase, block, everyone):
        arrival = gather_sem.at[phase // 4, block]

        @pl.when(my_block == block)
        def _():
            await_bytes(arrival, everyone.at[pl.ds(block * members, members - 1)])

        @pl.when(my_block != block)
        def _():
            await_bytes(arrival, everyone.at[pl.ds(block * members, members)])

    def gathered(everyone, first, last):
        places = range(first * members, last * members)
        return jnp.concatenate([everyone[place] for place in places], axis=1)

    def raise_block(block, everyone):
        left = gathered(everyone, block, block + 1)

        def one(step, carry):
            at = pl.multiple_of(step * batch, batch)
            part = lax.dot_general(
                left, table[pl.ds(at, batch), 2 * block * span : 2 * (block + 1) * span],
                (((1,), (1,)), ((), ())), preferred_element_type=F32,
            )
            acc[:, pl.ds(at, batch)] = part if block == 0 else acc[:, pl.ds(at, batch)] + part
            return carry

        lax.fori_loop(0, here // batch, one, 0)

    def raise_rest(phase, early, everyone, buffer, landing, norms, norm_src):
        wide = gathered(everyone, 0, blocks).astype(F32)
        norm_src[...] = jnp.broadcast_to(rows_to_lanes([lane_fold(wide * wide)]), (8, LANES))
        norms[me_f] = norm_src[...]

        def send(step, carry):
            to_feat(phase + 6, norm_src, norms.at[me_f], step).start()
            return carry

        lax.fori_loop(1, feats, send, 0)

        def one(index, carry):
            step = index + 1
            target = lax.rem(me_f + step, feats)
            at = pl.multiple_of(target * share, share)
            images = acc[:, pl.ds(at, share)] + lax.dot_general(
                gathered(everyone, early, blocks),
                table[pl.ds(at, share), 2 * early * span : 2 * width],
                (((1,), (1,)), ((), ())), preferred_element_type=F32,
            )
            buffer[target] = images

            @pl.when(step < feats)
            def _():
                to_feat(phase, buffer.at[target], landing.at[step - 1], step).start()

            @pl.when(step == feats)
            def _():
                i_part[...] = images

            return carry

        lax.fori_loop(0, feats, one, 0)
        await_bytes(recv_sem.at[phase + 6], norms.at[pl.ds(0, feats - 1)])
        squares = norms[0, 0:1, :]
        for part in range(1, feats):
            squares = squares + norms[part, 0:1, :]
        await_bytes(recv_sem.at[phase], landing)
        total = i_part[...]
        for slot in range(feats - 1):
            total = total + landing[slot]
        return total, lanes_to_rows(squares, 0, sides)

    def share_feats(phase, source, everyone, value):
        source[...] = value
        everyone[me_f] = value

        def send(step, carry):
            to_feat(phase, source, everyone.at[me_f], step).start()
            return carry

        lax.fori_loop(1, feats, send, 0)

    def await_feats(phase, everyone):
        await_bytes(recv_sem.at[phase], everyone.at[pl.ds(0, feats - 1)])
        return jnp.concatenate([everyone[part] for part in range(feats)], axis=1)

    early = max(1, blocks - 2)

    def own_first(block):
        @pl.when(my_block == block)
        def _():
            total, extra = collect(0, c_recv, c_send)
            c_own[0:sides, :] = total
            c_own[sides : sides + 8, :] = jnp.broadcast_to(extra, (8, LANES))
            share_rows(1, block, a_src, c_all, total.astype(BF16))

    make_block(0)
    project(0, c_send)
    make_block(1)
    pl.semaphore_wait(barrier, rows + feats - 2)
    ship(0, 0, c_send, c_recv)
    project(1, c_send)
    ship(0, 1, c_send, c_recv)
    for block in range(2, blocks):
        make_block(block)
        project(block, c_send)
        ship(0, block, c_send, c_recv)
        own_first(block - 2)
    own_first(blocks - 2)
    for block in range(early):
        await_block(0, block, c_all)
        raise_block(block, c_all)
        if block == 0:
            own_first(blocks - 1)
    for block in range(early, blocks):
        await_block(0, block, c_all)
    total, squares = raise_rest(2, early, c_all, i_send, i_recv, g_all, e_src)
    i_own[...] = total
    share_feats(3, b_src, i_all, total.astype(BF16))
    energy = lanes_to_rows(c_own[sides : sides + 1, :], 0, sides)
    alpha0 = energy / (squares + energy)
    images = await_feats(3, i_all)
    lhs[...] = images
    residual = (1.0 - alpha0) * rhs[...] - alpha0 * images.astype(F32)
    tail = rows_to_lanes([lane_fold(residual * residual), lane_fold(residual * rhs[...])])
    set_tail(s_send, spread(tail, 0, (16, LANES)).astype(BF16))

    def own_second(block):
        @pl.when(my_block == block)
        def _():
            total, extra = collect(4, s_recv, s_send)
            beta = lanes_to_rows(extra, 0, sides) / energy
            total = (1.0 - alpha0 + beta) * c_own[0:sides, :] - alpha0 * total
            c_own[sides : sides + 8, :] = jnp.broadcast_to(extra, (8, LANES))
            share_rows(5, block, c_src, d_all, total.astype(BF16))

    for block in range(blocks):
        project(block, s_send)
        ship(4, block, s_send, s_recv)
        if block >= 2:
            own_second(block - 2)
    if blocks == 2:
        own_second(0)
    for block in range(early):
        await_block(4, block, d_all)
        raise_block(block, d_all)
        if block == 0:
            for late in range(early, blocks):
                own_second(late)
    for block in range(early, blocks):
        await_block(4, block, d_all)
    total, squares = raise_rest(6, early, d_all, j_send, j_recv, h_all, f_src)
    energy_next = lanes_to_rows(c_own[sides : sides + 1, :], 0, sides)
    cross = lanes_to_rows(c_own[sides : sides + 1, :], sides, sides)
    beta = energy_next / energy
    direction_energy = energy_next + beta * (2.0 * cross + beta * energy)
    alpha1 = energy_next / (squares + direction_energy)

    mine = rhs[:, pl.ds(pl.multiple_of(me_f * share, share), share)]
    residual = (1.0 - alpha0) * mine - alpha0 * i_own[...]
    residual = residual - alpha1 * (total + residual + beta * mine)
    share_feats(7, d_src, j_all, residual.astype(BF16))
    right = rhs[...]
    residual = (1.0 - alpha0) * right - alpha0 * lhs[...].astype(F32)
    x_out[...] = alpha0 * right + alpha1 * (residual + beta * right)
    r_out[...] = await_feats(7, j_all).astype(F32)

    for phase, ref in (
        (0, c_recv), (1, c_all.at[pl.ds(0, rows - 1)]),
        (2, i_recv), (3, i_all.at[pl.ds(0, feats - 1)]),
        (4, s_recv), (5, d_all.at[pl.ds(0, rows - 1)]),
        (6, j_recv), (7, j_all.at[pl.ds(0, feats - 1)]),
        (8, g_all.at[pl.ds(0, feats - 1)]), (12, h_all.at[pl.ds(0, feats - 1)]),
    ):
        await_bytes(send_sem.at[phase], ref)


def block_count(rows):
    return 4 if rows % 8 == 0 else 2


def local(sizes, points, freq_index, log_density, targets, probes):
    rows, feats = sizes
    here = points.shape[1]
    width = freq_index.shape[1]
    sides = probes.shape[0] + 1
    share = here // feats
    vmem = pl.BlockSpec(memory_space=pltpu.VMEM)
    out = jax.ShapeDtypeStruct((sides, here), F32)
    block = (sides + 16, LANES)
    scratch = [
        pltpu.VMEM((here, 2 * width), BF16),
        pltpu.VMEM((here, 32), BF16),
        pltpu.VMEM((sides, here), F32),
        pltpu.VMEM((sides, here), BF16),
        pltpu.VMEM((sides, here), F32),
        pltpu.VMEM((sides, LANES), F32),
        pltpu.VMEM((rows, *block), BF16),
        pltpu.VMEM((rows - 1, *block), BF16),
        pltpu.VMEM((sides + 8, LANES), F32),
        pltpu.VMEM((rows, sides, LANES), BF16),
        pltpu.VMEM((rows, *block), BF16),
        pltpu.VMEM((rows - 1, *block), BF16),
        pltpu.VMEM((rows, sides, LANES), BF16),
        pltpu.VMEM((sides, share), F32),
        pltpu.VMEM((sides, share), F32),
        pltpu.VMEM((feats, sides, share), F32),
        pltpu.VMEM((feats - 1, sides, share), F32),
        pltpu.VMEM((feats, sides, share), BF16),
        pltpu.VMEM((feats, sides, share), F32),
        pltpu.VMEM((feats - 1, sides, share), F32),
        pltpu.VMEM((feats, sides, share), BF16),
        pltpu.VMEM((feats, 8, LANES), F32),
        pltpu.VMEM((feats, 8, LANES), F32),
        pltpu.VMEM((sides, LANES), BF16),
        pltpu.VMEM((sides, share), BF16),
        pltpu.VMEM((sides, LANES), BF16),
        pltpu.VMEM((sides, share), BF16),
        pltpu.VMEM((8, LANES), F32),
        pltpu.VMEM((8, LANES), F32),
        pltpu.SemaphoreType.DMA((13,)),
        pltpu.SemaphoreType.DMA((13,)),
        pltpu.SemaphoreType.DMA((2, block_count(rows))),
    ]
    return pl.pallas_call(
        functools.partial(kernel, sizes),
        out_shape=(out, out),
        in_specs=[vmem] * 5,
        out_specs=(vmem, vmem),
        scratch_shapes=scratch,
        name="regress",
        compiler_params=pltpu.CompilerParams(
            collective_id=0, has_side_effects=True, vmem_limit_bytes=56 << 20
        ),
    )(points, freq_index, log_density.reshape(1, width), targets.reshape(1, here), probes)


def solution(mesh):
    sizes = (mesh.shape["rows"], mesh.shape["feat"])
    in_specs = (P(None, "rows"), P(None, "feat"), P("feat"), P("rows"), P(None, "rows"))
    out_specs = (P(None, "rows"), P(None, "rows"))
    return jax.shard_map(
        functools.partial(local, sizes),
        mesh=mesh, in_specs=in_specs, out_specs=out_specs, check_vma=False,
    )
```

time: 145 us -> 121 us (0.83)
  Pallas kernels: 141 us -> 117 us
    pallas_call x1, Pallas kernels: 141 us -> 117 us  [local(): pl.pallas_call(functools.partial(kernel, sizes), out_shape=(out, out), in...]
where the time goes in v2:
time: 121 us
  Pallas kernels  117 us (97%)
  local copies, waits for them, and re-layouts  2.72 us (2%)
    pallas_call x1, Pallas kernels, local(): pl.pallas_call(functools.partial(kernel, sizes), out_shape=(out, out), in...  117 us
    unnamed x4, local copies, waits for them, and re-layouts  2.72 us

profile of v2, /device:TPU:1, one launch (start us, length us, event | category | flops | bytes accessed | tf_op | source)
XLA Modules:
  0.0 120.7 jit_solution(15007381860019723010)
XLA Ops:
  0.6 117.4 %regress.1 = (f32[32,4096]{1,0:T(8,128)}, f32[32,4096]{1,0:T(8,128)}) custom-call(f32[8,4096]{1,0:T(8,128)} %points.1, s32[8,2048]{1,0:T(8,128)} %freq.1, f32[1,2048]{1,0:T(1,128)} %bitcast.3, f32[1,4096]{1,0:T(1,128)} %bitcast.2, s32[31,4096]{1,0:T(8,128)} %probes.1), custom_call_target="tpu_custom_call" | custom-call | tf_op jit(solution)/shard_map/regress/pallas_call | solution.py:435
  118.0 0.0 copy-start
  118.0 1.9 %copy.9 = f32[32,4096]{1,0:T(8,128)} copy(f32[32,4096]{1,0:T(8,128)} %get-tuple-element.4) | data formatting | bytes 1048576
  119.9 0.0 copy-done
  119.9 0.8 copy.10
Async XLA Ops:
  118.0 1.9 %copy-start = (f32[32,4096]{1,0:T(8,128)S(1)}, f32[32,4096]{1,0:T(8,128)}, u32[]{:S(2)}) copy-start(f32[32,4096]{1,0:T(8,128)} %get-tuple-element.5) | copy-start | bytes 1572868

commit v3 on v2

--- a/solution.py
+++ b/solution.py
@@ -1,5 +1,6 @@
 import functools
 import math
+from types import SimpleNamespace
 
 import jax
 import jax.numpy as jnp
@@ -38,16 +39,6 @@
     return high, middle, value - high - middle
 
 
-def spread(value, axis, shape):
-    high, middle, low = three_way(value)
-    place = lax.broadcasted_iota(jnp.int32, shape, axis)
-    high, middle, low = (jnp.broadcast_to(part, shape) for part in (high, middle, low))
-    zero = jnp.zeros(shape, F32)
-    return jnp.where(
-        place == 0, high, jnp.where(place == 1, middle, jnp.where(place == 2, low, zero))
-    )
-
-
 def lane_fold(value):
     total = value[:, :LANES]
     for start in range(LANES, value.shape[1], LANES):
@@ -75,7 +66,8 @@
     table, turns_t, rhs, lhs, acc,
     c_part, c_send, c_recv, c_own, c_all, s_send, s_recv, d_all,
     i_part, i_own, i_send, i_recv, i_all, j_send, j_recv, j_all, g_all, h_all,
-    a_src, b_src, c_src, d_src, e_src, f_src, send_sem, recv_sem, gather_sem,
+    a_src, b_src, c_src, d_src, e_src, f_src, z_send, cz_recv, sz_recv,
+    e_sums, ex_sums, e_sums_x, ez_sums, e_all, n_sums, nx_sums, n_sums_x, nz_sums, n_all, send_sem, recv_sem, gather_sem,
 ):
     rows, feats = sizes
     me_r = lax.axis_index("rows")
@@ -88,8 +80,9 @@
     members = rows // blocks
     span = width // blocks
     batch = min(1024, here)
+    my_member = me_r // blocks
     my_block = lax.rem(me_r, blocks)
-    my_place = my_block * members + me_r // blocks
+    my_place = my_block * members + my_member
 
     barrier = pltpu.get_barrier_semaphore()
 
@@ -108,10 +101,18 @@
     lax.fori_loop(1, rows, greet_row, 0)
     lax.fori_loop(1, feats, greet_feat, 0)
 
-    def to_row(phase, arrival, src, dst, step):
+    def across(phase, arrival, src, dst, step):
+        target = my_member * blocks + lax.rem(my_block + step, blocks)
         return pltpu.make_async_remote_copy(
             src_ref=src, dst_ref=dst, send_sem=send_sem.at[phase], recv_sem=arrival,
-            device_id=(lax.rem(me_r + step, rows), me_f), device_id_type=MESH,
+            device_id=(target, me_f), device_id_type=MESH,
+        )
+
+    def along(phase, arrival, src, dst, step):
+        target = lax.rem(my_member + step, members) * blocks + my_block
+        return pltpu.make_async_remote_copy(
+            src_ref=src, dst_ref=dst, send_sem=send_sem.at[phase], recv_sem=arrival,
+            device_id=(target, me_f), device_id_type=MESH,
         )
 
     def to_feat(phase, src, dst, step):
@@ -130,16 +131,7 @@
     high, middle, low = three_way(points[...] * TURN)
     stacked = jnp.concatenate([high, middle, low, jnp.zeros_like(high)], axis=0)
     turns_t[...] = stacked.T.astype(BF16)
-    tail = spread(rows_to_lanes([lane_fold(right * right)]), 0, (16, LANES)).astype(BF16)
-
-    def set_tail(buffer, tail):
-        def put(chunk, carry):
-            buffer[chunk, sides : sides + 16, :] = tail
-            return carry
-
-        lax.fori_loop(0, rows, put, 0)
-
-    set_tail(c_send, tail)
+    e_sums[0] = rows_to_lanes([lane_fold(right * right)])
 
     def make_block(block):
         at = block * span
@@ -164,78 +156,123 @@
             for piece in range(span // LANES):
                 member = part * (members // 2) + piece
                 value = sums[:, piece * LANES : (piece + 1) * LANES]
-                buffer[block * members + member, 0:sides, :] = value.astype(BF16)
-
-                @pl.when(me_r == member * blocks + block)
+                buffer[block * members + member] = value.astype(BF16)
+
+                @pl.when(my_block == block)
                 def _():
-                    c_part[...] = value
-
-    def ship(phase, block, buffer, landing):
-        def send(member, carry):
-            step = lax.rem(member * blocks + block + rows - me_r, rows)
-
-            @pl.when(step != 0)
-            def _():
-                to_row(
-                    phase, recv_sem.at[phase], buffer.at[block * members + member],
-                    landing.at[step - 1], step,
-                ).start()
-
-            return carry
-
-        lax.fori_loop(0, members, send, 0)
-
-    def collect(phase, landing, buffer):
-        await_bytes(recv_sem.at[phase], landing)
-
-        def add(slot, carry):
-            total, extra = carry
-            total = total + landing[slot, 0:sides, :].astype(F32)
-            return total, extra + landing[slot, sides : sides + 16, :].astype(F32)
-
-        first = (c_part[...], buffer[0, sides : sides + 16, :].astype(F32))
-        total, extra = lax.fori_loop(0, rows - 1, add, first)
-        return total, jnp.sum(extra, axis=0, keepdims=True)
-
-    def share_rows(phase, block, source, everyone, value):
-        source[...] = value
-        everyone[my_place] = value
-
-        def send(step, carry):
-            arrival = gather_sem.at[phase // 4, block]
-            to_row(phase, arrival, source, everyone.at[my_place], step).start()
-            return carry
-
-        lax.fori_loop(1, rows, send, 0)
-
-    def await_block(phase, block, everyone):
-        arrival = gather_sem.at[phase // 4, block]
-
+                    c_part[member] = value
+
+    def ship(block, kit):
+        step = lax.rem(block + blocks - my_block, blocks)
+
+        @pl.when(step != 0)
+        def _():
+            phase = kit.phase
+            source = kit.send.at[pl.ds(block * members, members)]
+            across(phase, recv_sem.at[phase], source, kit.x_recv.at[step - 1], step).start()
+            sums = kit.x_sums.at[pl.ds(step - 1, 1)]
+            across(phase + 1, recv_sem.at[phase + 1], kit.sums, sums, step).start()
+
+    def stage_two(block, kit):
         @pl.when(my_block == block)
         def _():
-            await_bytes(arrival, everyone.at[pl.ds(block * members, members - 1)])
-
+            phase = kit.phase
+            await_bytes(recv_sem.at[phase], kit.x_recv)
+            await_bytes(recv_sem.at[phase + 1], kit.x_sums)
+            total = kit.sums[0]
+            for slot in range(blocks - 1):
+                total = total + kit.x_sums[slot]
+            kit.sums_x[0] = total
+
+            def add(member, carry):
+                value = c_part[member]
+                for slot in range(blocks - 1):
+                    value = value + kit.x_recv[slot, member].astype(F32)
+                z_send[member] = value
+                return carry
+
+            lax.fori_loop(0, members, add, 0)
+
+            def send(step, carry):
+                source = z_send.at[lax.rem(my_member + step, members)]
+                along(phase + 2, recv_sem.at[phase + 2], source, kit.z_recv.at[step - 1], step).start()
+                sums = kit.z_sums.at[pl.ds(step - 1, 1)]
+                along(phase + 3, recv_sem.at[phase + 3], kit.sums_x, sums, step).start()
+                return carry
+
+            lax.fori_loop(1, members, send, 0)
+
+    def stage_three(block, kit, finish):
+        @pl.when(my_block == block)
+        def _():
+            phase = kit.phase
+            await_bytes(recv_sem.at[phase + 2], kit.z_recv)
+            await_bytes(recv_sem.at[phase + 3], kit.z_sums)
+            sums = kit.sums_x[0]
+            for slot in range(members - 1):
+                sums = sums + kit.z_sums[slot]
+            kit.sums_all[...] = sums
+            total = z_send[my_member]
+            for slot in range(members - 1):
+                total = total + kit.z_recv[slot]
+            value = finish(total, sums).astype(BF16)
+            kit.source[...] = value
+            kit.everyone[my_place] = value
+
+            def send(step, carry):
+                target = kit.everyone.at[my_place]
+                along(phase + 4, recv_sem.at[phase + 4], kit.source, target, step).start()
+                return carry
+
+            lax.fori_loop(1, members, send, 0)
+            await_bytes(send_sem.at[phase + 2], kit.z_recv)
+
+    def stage_four(block, kit):
+        @pl.when(my_block == block)
+        def _():
+            phase = kit.phase
+            await_bytes(recv_sem.at[phase + 4], kit.everyone.at[pl.ds(0, members - 1)])
+            whole = kit.everyone.at[pl.ds(block * members, members)]
+
+            def send(step, carry):
+                across(phase + 5, gather_sem.at[kit.turn, block], whole, whole, step).start()
+                return carry
+
+            lax.fori_loop(1, blocks, send, 0)
+
+    def await_block(block, kit):
         @pl.when(my_block != block)
         def _():
-            await_bytes(arrival, everyone.at[pl.ds(block * members, members)])
+            region = kit.everyone.at[pl.ds(block * members, members)]
+            await_bytes(gather_sem.at[kit.turn, block], region)
+
+    def finish_rows(kit):
+        phase = kit.phase
+        await_bytes(send_sem.at[phase], kit.x_recv)
+        await_bytes(send_sem.at[phase + 1], kit.x_sums)
+        await_bytes(send_sem.at[phase + 3], kit.z_sums)
+        await_bytes(send_sem.at[phase + 4], kit.everyone.at[pl.ds(0, members - 1)])
+        await_bytes(send_sem.at[phase + 5], kit.everyone.at[pl.ds(0, (blocks - 1) * members)])
 
     def gathered(everyone, first, last):
         places = range(first * members, last * members)
         return jnp.concatenate([everyone[place] for place in places], axis=1)
 
-    def raise_block(block, everyone):
+    def raise_block(block, everyone, half):
         left = gathered(everyone, block, block + 1)
+        slab = min(1024, here // 2)
+        count = here // slab // 2
 
         def one(step, carry):
-            at = pl.multiple_of(step * batch, batch)
+            at = pl.multiple_of(step * slab, slab)
             part = lax.dot_general(
-                left, table[pl.ds(at, batch), 2 * block * span : 2 * (block + 1) * span],
+                left, table[pl.ds(at, slab), 2 * block * span : 2 * (block + 1) * span],
                 (((1,), (1,)), ((), ())), preferred_element_type=F32,
             )
-            acc[:, pl.ds(at, batch)] = part if block == 0 else acc[:, pl.ds(at, batch)] + part
+            acc[:, pl.ds(at, slab)] = part if block == 0 else acc[:, pl.ds(at, slab)] + part
             return carry
 
-        lax.fori_loop(0, here // batch, one, 0)
+        lax.fori_loop(half * count, (half + 1) * count, one, 0)
 
     def raise_rest(phase, early, everyone, buffer, landing, norms, norm_src):
         wide = gathered(everyone, 0, blocks).astype(F32)
@@ -294,74 +331,104 @@
         await_bytes(recv_sem.at[phase], everyone.at[pl.ds(0, feats - 1)])
         return jnp.concatenate([everyone[part] for part in range(feats)], axis=1)
 
-    early = max(1, blocks - 2)
-
-    def own_first(block):
-        @pl.when(my_block == block)
-        def _():
-            total, extra = collect(0, c_recv, c_send)
-            c_own[0:sides, :] = total
-            c_own[sides : sides + 8, :] = jnp.broadcast_to(extra, (8, LANES))
-            share_rows(1, block, a_src, c_all, total.astype(BF16))
-
+    early = blocks - 1
+    one_kit = SimpleNamespace(
+        phase=16, turn=0, send=c_send, x_recv=c_recv, z_recv=cz_recv, everyone=c_all, source=a_src,
+        sums=e_sums, x_sums=ex_sums, sums_x=e_sums_x, z_sums=ez_sums, sums_all=e_all,
+    )
+    two_kit = SimpleNamespace(
+        phase=22, turn=1, send=s_send, x_recv=s_recv, z_recv=sz_recv, everyone=d_all, source=c_src,
+        sums=n_sums, x_sums=nx_sums, sums_x=n_sums_x, z_sums=nz_sums, sums_all=n_all,
+    )
+
+    def keep_first(total, sums):
+        c_own[...] = total
+        return total
+
+    kit = one_kit
     make_block(0)
     project(0, c_send)
     make_block(1)
     pl.semaphore_wait(barrier, rows + feats - 2)
-    ship(0, 0, c_send, c_recv)
+    ship(0, kit)
     project(1, c_send)
-    ship(0, 1, c_send, c_recv)
-    for block in range(2, blocks):
-        make_block(block)
-        project(block, c_send)
-        ship(0, block, c_send, c_recv)
-        own_first(block - 2)
-    own_first(blocks - 2)
-    for block in range(early):
-        await_block(0, block, c_all)
-        raise_block(block, c_all)
-        if block == 0:
-            own_first(blocks - 1)
-    for block in range(early, blocks):
-        await_block(0, block, c_all)
+    ship(1, kit)
+    make_block(2)
+    stage_two(0, kit)
+    project(2, c_send)
+    ship(2, kit)
+    stage_three(0, kit, keep_first)
+    stage_two(1, kit)
+    make_block(3)
+    stage_four(0, kit)
+    stage_three(1, kit, keep_first)
+    stage_two(2, kit)
+    project(3, c_send)
+    ship(3, kit)
+    stage_four(1, kit)
+    stage_three(2, kit, keep_first)
+    await_block(0, kit)
+    raise_block(0, c_all, 0)
+    raise_block(0, c_all, 1)
+    stage_four(2, kit)
+    stage_two(3, kit)
+    await_block(1, kit)
+    raise_block(1, c_all, 0)
+    raise_block(1, c_all, 1)
+    stage_three(3, kit, keep_first)
+    await_block(2, kit)
+    raise_block(2, c_all, 0)
+    stage_four(3, kit)
+    raise_block(2, c_all, 1)
+    await_block(3, kit)
     total, squares = raise_rest(2, early, c_all, i_send, i_recv, g_all, e_src)
     i_own[...] = total
     share_feats(3, b_src, i_all, total.astype(BF16))
-    energy = lanes_to_rows(c_own[sides : sides + 1, :], 0, sides)
+    energy = lanes_to_rows(e_all[...], 0, sides)
     alpha0 = energy / (squares + energy)
     images = await_feats(3, i_all)
     lhs[...] = images
     residual = (1.0 - alpha0) * rhs[...] - alpha0 * images.astype(F32)
-    tail = rows_to_lanes([lane_fold(residual * residual), lane_fold(residual * rhs[...])])
-    set_tail(s_send, spread(tail, 0, (16, LANES)).astype(BF16))
-
-    def own_second(block):
-        @pl.when(my_block == block)
-        def _():
-            total, extra = collect(4, s_recv, s_send)
-            beta = lanes_to_rows(extra, 0, sides) / energy
-            total = (1.0 - alpha0 + beta) * c_own[0:sides, :] - alpha0 * total
-            c_own[sides : sides + 8, :] = jnp.broadcast_to(extra, (8, LANES))
-            share_rows(5, block, c_src, d_all, total.astype(BF16))
-
-    for block in range(blocks):
-        project(block, s_send)
-        ship(4, block, s_send, s_recv)
-        if block >= 2:
-            own_second(block - 2)
-    if blocks == 2:
-        own_second(0)
-    for block in range(early):
-        await_block(4, block, d_all)
-        raise_block(block, d_all)
-        if block == 0:
-            for late in range(early, blocks):
-                own_second(late)
-    for block in range(early, blocks):
-        await_block(4, block, d_all)
+    n_sums[0] = rows_to_lanes([lane_fold(residual * residual), lane_fold(residual * rhs[...])])
+
+    def combine(total, sums):
+        beta = lanes_to_rows(sums, 0, sides) / energy
+        return (1.0 - alpha0 + beta) * c_own[...] - alpha0 * total
+
+    kit = two_kit
+    project(0, s_send)
+    ship(0, kit)
+    project(1, s_send)
+    ship(1, kit)
+    stage_two(0, kit)
+    project(2, s_send)
+    ship(2, kit)
+    stage_three(0, kit, combine)
+    stage_two(1, kit)
+    project(3, s_send)
+    ship(3, kit)
+    stage_four(0, kit)
+    stage_three(1, kit, combine)
+    stage_two(2, kit)
+    await_block(0, kit)
+    raise_block(0, d_all, 0)
+    stage_four(1, kit)
+    stage_three(2, kit, combine)
+    raise_block(0, d_all, 1)
+    stage_two(3, kit)
+    await_block(1, kit)
+    raise_block(1, d_all, 0)
+    stage_four(2, kit)
+    raise_block(1, d_all, 1)
+    stage_three(3, kit, combine)
+    await_block(2, kit)
+    raise_block(2, d_all, 0)
+    stage_four(3, kit)
+    raise_block(2, d_all, 1)
+    await_block(3, kit)
     total, squares = raise_rest(6, early, d_all, j_send, j_recv, h_all, f_src)
-    energy_next = lanes_to_rows(c_own[sides : sides + 1, :], 0, sides)
-    cross = lanes_to_rows(c_own[sides : sides + 1, :], sides, sides)
+    energy_next = lanes_to_rows(n_all[...], 0, sides)
+    cross = lanes_to_rows(n_all[...], sides, sides)
     beta = energy_next / energy
     direction_energy = energy_next + beta * (2.0 * cross + beta * energy)
     alpha1 = energy_next / (squares + direction_energy)
@@ -376,17 +443,17 @@
     r_out[...] = await_feats(7, j_all).astype(F32)
 
     for phase, ref in (
-        (0, c_recv), (1, c_all.at[pl.ds(0, rows - 1)]),
         (2, i_recv), (3, i_all.at[pl.ds(0, feats - 1)]),
-        (4, s_recv), (5, d_all.at[pl.ds(0, rows - 1)]),
         (6, j_recv), (7, j_all.at[pl.ds(0, feats - 1)]),
         (8, g_all.at[pl.ds(0, feats - 1)]), (12, h_all.at[pl.ds(0, feats - 1)]),
     ):
         await_bytes(send_sem.at[phase], ref)
+    finish_rows(one_kit)
+    finish_rows(two_kit)
 
 
 def block_count(rows):
-    return 4 if rows % 8 == 0 else 2
+    return 4
 
 
 def local(sizes, points, freq_index, log_density, targets, probes):
@@ -397,20 +464,22 @@
     share = here // feats
     vmem = pl.BlockSpec(memory_space=pltpu.VMEM)
     out = jax.ShapeDtypeStruct((sides, here), F32)
-    block = (sides + 16, LANES)
+    block = (sides, LANES)
+    blocks = block_count(rows)
+    members = rows // blocks
     scratch = [
         pltpu.VMEM((here, 2 * width), BF16),
         pltpu.VMEM((here, 32), BF16),
         pltpu.VMEM((sides, here), F32),
         pltpu.VMEM((sides, here), BF16),
         pltpu.VMEM((sides, here), F32),
+        pltpu.VMEM((members, *block), F32),
+        pltpu.VMEM((rows, *block), BF16),
+        pltpu.VMEM((blocks - 1, members, *block), BF16),
         pltpu.VMEM((sides, LANES), F32),
-        pltpu.VMEM((rows, *block), BF16),
-        pltpu.VMEM((rows - 1, *block), BF16),
-        pltpu.VMEM((sides + 8, LANES), F32),
         pltpu.VMEM((rows, sides, LANES), BF16),
         pltpu.VMEM((rows, *block), BF16),
-        pltpu.VMEM((rows - 1, *block), BF16),
+        pltpu.VMEM((blocks - 1, members, *block), BF16),
         pltpu.VMEM((rows, sides, LANES), BF16),
         pltpu.VMEM((sides, share), F32),
         pltpu.VMEM((sides, share), F32),
@@ -428,8 +497,18 @@
         pltpu.VMEM((sides, share), BF16),
         pltpu.VMEM((8, LANES), F32),
         pltpu.VMEM((8, LANES), F32),
-        pltpu.SemaphoreType.DMA((13,)),
-        pltpu.SemaphoreType.DMA((13,)),
+        pltpu.VMEM((members, *block), F32),
+        pltpu.VMEM((members - 1, *block), F32),
+        pltpu.VMEM((members - 1, *block), F32),
+    ] + 2 * [
+        pltpu.VMEM((1, 1, LANES), F32),
+        pltpu.VMEM((blocks - 1, 1, LANES), F32),
+        pltpu.VMEM((1, 1, LANES), F32),
+        pltpu.VMEM((members - 1, 1, LANES), F32),
+        pltpu.VMEM((1, LANES), F32),
+    ] + [
+        pltpu.SemaphoreType.DMA((28,)),
+        pltpu.SemaphoreType.DMA((28,)),
         pltpu.SemaphoreType.DMA((2, block_count(rows))),
     ]
     return pl.pallas_call(

time: 121 us -> 136 us (1.12)
  Pallas kernels: 117 us -> 132 us
    pallas_call x1, Pallas kernels: 117 us -> 132 us  [local(): pl.pallas_call(functools.partial(kernel, sizes), out_shape=(out, out), in...]
where the time goes in v3:
time: 136 us
  Pallas kernels  132 us (97%)
  local copies, waits for them, and re-layouts  2.72 us (2%)
    pallas_call x1, Pallas kernels, local(): pl.pallas_call(functools.partial(kernel, sizes), out_shape=(out, out), in...  132 us
    unnamed x4, local copies, waits for them, and re-layouts  2.72 us

profile of v3, /device:TPU:1, one launch (start us, length us, event | category | flops | bytes accessed | tf_op | source)
XLA Modules:
  0.0 135.6 jit_solution(10984901138728758736)
XLA Ops:
  0.6 132.2 %regress.1 = (f32[32,4096]{1,0:T(8,128)}, f32[32,4096]{1,0:T(8,128)}) custom-call(f32[8,4096]{1,0:T(8,128)} %points.1, s32[8,2048]{1,0:T(8,128)} %freq.1, f32[1,2048]{1,0:T(1,128)} %bitcast.3, f32[1,4096]{1,0:T(1,128)} %bitcast.2, s32[31,4096]{1,0:T(8,128)} %probes.1), custom_call_target="tpu_custom_call" | custom-call | tf_op jit(solution)/shard_map/regress/pallas_call | solution.py:514
  132.9 0.0 copy-start
  132.9 1.9 %copy.9 = f32[32,4096]{1,0:T(8,128)} copy(f32[32,4096]{1,0:T(8,128)} %get-tuple-element.4) | data formatting | bytes 1048576
  134.8 0.0 copy-done
  134.8 0.8 copy.10
Async XLA Ops:
  132.9 1.9 %copy-start = (f32[32,4096]{1,0:T(8,128)S(1)}, f32[32,4096]{1,0:T(8,128)}, u32[]{:S(2)}) copy-start(f32[32,4096]{1,0:T(8,128)} %get-tuple-element.5) | copy-start | bytes 1572868

commit v4 on v2

--- a/solution.py
+++ b/solution.py
@@ -87,9 +87,15 @@
     blocks = block_count(rows)
     members = rows // blocks
     span = width // blocks
-    batch = min(1024, here)
-    my_block = lax.rem(me_r, blocks)
-    my_place = my_block * members + me_r // blocks
+    batch = min(2048, here)
+    sub = max(LANES, span // 2)
+    my_member = me_r // blocks
+    my_block = lax.rem(me_r + my_member, blocks)
+    my_place = my_block * members + my_member
+
+    def owner(block, member):
+        return member * blocks + lax.rem(block + members * blocks - member, blocks)
+
 
     barrier = pltpu.get_barrier_semaphore()
 
@@ -147,32 +153,68 @@
         whole = jnp.concatenate([whole, whole, whole, jnp.zeros_like(whole)], axis=0).astype(BF16)
         strength = jnp.exp(0.5 * density[:, at : at + span]) * (1.0 / math.sqrt(FREQS))
 
+        acc[:, 2 * at : 2 * (at + span)] = jnp.zeros((sides, 2 * span), F32)
+
         def fill(step, carry):
             first = pl.multiple_of(step * batch, batch)
-            turns = jnp.dot(turns_t[pl.ds(first, batch), :], whole, preferred_element_type=F32)
-            cosine, sine = scaled_trig(turns, strength)
-            table[pl.ds(first, batch), 2 * at : 2 * at + span] = cosine.astype(BF16)
-            table[pl.ds(first, batch), 2 * at + span : 2 * (at + span)] = sine.astype(BF16)
+            here_turns = turns_t[pl.ds(first, batch), :]
+            left = lhs[:, pl.ds(first, batch)]
+
+            def add(values, start):
+                acc[:, start : start + sub] += jnp.dot(left, values, preferred_element_type=F32)
+
+            pending = []
+            turns = jnp.dot(here_turns, whole[:, 0:sub], preferred_element_type=F32)
+            for start in range(0, span, sub):
+                later = start + sub
+                ahead = turns
+                if later < span:
+                    ahead = jnp.dot(
+                        here_turns, whole[:, later : later + sub], preferred_element_type=F32
+                    )
+                cosine, sine = scaled_trig(turns, strength[:, start : start + sub])
+                cosine = cosine.astype(BF16)
+                sine = sine.astype(BF16)
+                for values, place in pending:
+                    add(values, place)
+                table[pl.ds(first, batch), 2 * at + start : 2 * at + start + sub] = cosine
+                shifted = 2 * at + span + start
+                table[pl.ds(first, batch), shifted : shifted + sub] = sine
+                pending = [(cosine, 2 * at + start), (sine, shifted)]
+                turns = ahead
+            for values, place in pending:
+                add(values, place)
             return carry
 
         lax.fori_loop(0, here // batch, fill, 0)
 
-    def project(block, buffer):
+    def project(block, buffer, known=False):
         for part in range(2):
             at = (2 * block + part) * span
-            sums = jnp.dot(lhs[...], table[:, at : at + span], preferred_element_type=F32)
+            if known:
+                sums = acc[:, at : at + span]
+            else:
+                sums = acc[:, at : at + span]
+                for other in range(1, feats // 2):
+                    which = lax.rem(me_f // 2 + other, feats // 2)
+                    left = jnp.concatenate([i_all[2 * which], i_all[2 * which + 1]], axis=1)
+                    first = pl.multiple_of(which * (2 * share), 2 * share)
+                    sums = sums + jnp.dot(
+                        left, table[pl.ds(first, 2 * share), at : at + span],
+                        preferred_element_type=F32,
+                    )
             for piece in range(span // LANES):
                 member = part * (members // 2) + piece
                 value = sums[:, piece * LANES : (piece + 1) * LANES]
                 buffer[block * members + member, 0:sides, :] = value.astype(BF16)
 
-                @pl.when(me_r == member * blocks + block)
+                @pl.when(my_place == block * members + member)
                 def _():
                     c_part[...] = value
 
     def ship(phase, block, buffer, landing):
         def send(member, carry):
-            step = lax.rem(member * blocks + block + rows - me_r, rows)
+            step = lax.rem(owner(block, member) + rows - me_r, rows)
 
             @pl.when(step != 0)
             def _():
@@ -223,19 +265,21 @@
         places = range(first * members, last * members)
         return jnp.concatenate([everyone[place] for place in places], axis=1)
 
-    def raise_block(block, everyone):
+    def raise_block(block, everyone, half):
         left = gathered(everyone, block, block + 1)
+        slab = min(1024, here // 2)
+        count = here // slab // 2
 
         def one(step, carry):
-            at = pl.multiple_of(step * batch, batch)
+            at = pl.multiple_of(step * slab, slab)
             part = lax.dot_general(
-                left, table[pl.ds(at, batch), 2 * block * span : 2 * (block + 1) * span],
+                left, table[pl.ds(at, slab), 2 * block * span : 2 * (block + 1) * span],
                 (((1,), (1,)), ((), ())), preferred_element_type=F32,
             )
-            acc[:, pl.ds(at, batch)] = part if block == 0 else acc[:, pl.ds(at, batch)] + part
-            return carry
-
-        lax.fori_loop(0, here // batch, one, 0)
+            acc[:, pl.ds(at, slab)] = part if block == 0 else acc[:, pl.ds(at, slab)] + part
+            return carry
+
+        lax.fori_loop(half * count, (half + 1) * count, one, 0)
 
     def raise_rest(phase, early, everyone, buffer, landing, norms, norm_src):
         wide = gathered(everyone, 0, blocks).astype(F32)
@@ -249,8 +293,9 @@
         lax.fori_loop(1, feats, send, 0)
 
         def one(index, carry):
-            step = index + 1
-            target = lax.rem(me_f + step, feats)
+            pair = lax.rem(me_f // 2 + index // 2 + 1, feats // 2)
+            target = 2 * pair + lax.rem(me_f + 1 + index, 2)
+            step = lax.rem(target + feats - me_f, feats)
             at = pl.multiple_of(target * share, share)
             images = acc[:, pl.ds(at, share)] + lax.dot_general(
                 gathered(everyone, early, blocks),
@@ -259,11 +304,11 @@
             )
             buffer[target] = images
 
-            @pl.when(step < feats)
+            @pl.when(step != 0)
             def _():
                 to_feat(phase, buffer.at[target], landing.at[step - 1], step).start()
 
-            @pl.when(step == feats)
+            @pl.when(step == 0)
             def _():
                 i_part[...] = images
 
@@ -305,31 +350,61 @@
             share_rows(1, block, a_src, c_all, total.astype(BF16))
 
     make_block(0)
-    project(0, c_send)
+    project(0, c_send, True)
     make_block(1)
     pl.semaphore_wait(barrier, rows + feats - 2)
     ship(0, 0, c_send, c_recv)
-    project(1, c_send)
+    project(1, c_send, True)
     ship(0, 1, c_send, c_recv)
     for block in range(2, blocks):
         make_block(block)
-        project(block, c_send)
+        project(block, c_send, True)
         ship(0, block, c_send, c_recv)
         own_first(block - 2)
     own_first(blocks - 2)
     for block in range(early):
         await_block(0, block, c_all)
-        raise_block(block, c_all)
+        raise_block(block, c_all, 0)
         if block == 0:
             own_first(blocks - 1)
+        raise_block(block, c_all, 1)
     for block in range(early, blocks):
         await_block(0, block, c_all)
     total, squares = raise_rest(2, early, c_all, i_send, i_recv, g_all, e_src)
     i_own[...] = total
-    share_feats(3, b_src, i_all, total.astype(BF16))
+    b_src[...] = total.astype(BF16)
+    i_all[me_f] = b_src[...]
+    chip = me_f // 2
+    to_sibling = lax.rem(2 * chip + lax.rem(me_f + 1, 2) + feats - me_f, feats)
+
+    def send_far(step, carry):
+        @pl.when(step != to_sibling)
+        def _():
+            to_feat(3, b_src, i_all.at[me_f], step).start()
+
+        return carry
+
+    lax.fori_loop(1, feats, send_far, 0)
+    to_feat(11, b_src, i_all.at[me_f], to_sibling).start()
     energy = lanes_to_rows(c_own[sides : sides + 1, :], 0, sides)
     alpha0 = energy / (squares + energy)
-    images = await_feats(3, i_all)
+    await_bytes(recv_sem.at[11], i_all.at[pl.ds(0, 1)])
+
+    def pair_of(which):
+        return jnp.concatenate([i_all[2 * which], i_all[2 * which + 1]], axis=1)
+
+    def rows_of(which):
+        return pl.ds(pl.multiple_of(which * (2 * share), 2 * share), 2 * share)
+
+    near = pair_of(chip)
+    for part in range(2 * blocks):
+        at = part * span
+        acc[:, at : at + span] = jnp.dot(
+            near, table[rows_of(chip), at : at + span], preferred_element_type=F32
+        )
+    if feats > 2:
+        await_bytes(recv_sem.at[3], i_all.at[pl.ds(0, feats - 2)])
+    images = jnp.concatenate([i_all[part] for part in range(feats)], axis=1)
     lhs[...] = images
     residual = (1.0 - alpha0) * rhs[...] - alpha0 * images.astype(F32)
     tail = rows_to_lanes([lane_fold(residual * residual), lane_fold(residual * rhs[...])])
@@ -353,10 +428,12 @@
         own_second(0)
     for block in range(early):
         await_block(4, block, d_all)
-        raise_block(block, d_all)
+        if block == 0 and blocks > 2:
+            own_second(blocks - 2)
+        raise_block(block, d_all, 0)
         if block == 0:
-            for late in range(early, blocks):
-                own_second(late)
+            own_second(blocks - 1)
+        raise_block(block, d_all, 1)
     for block in range(early, blocks):
         await_block(4, block, d_all)
     total, squares = raise_rest(6, early, d_all, j_send, j_recv, h_all, f_src)
@@ -377,12 +454,14 @@
 
     for phase, ref in (
         (0, c_recv), (1, c_all.at[pl.ds(0, rows - 1)]),
-        (2, i_recv), (3, i_all.at[pl.ds(0, feats - 1)]),
+        (2, i_recv), (11, i_all.at[pl.ds(0, 1)]),
         (4, s_recv), (5, d_all.at[pl.ds(0, rows - 1)]),
         (6, j_recv), (7, j_all.at[pl.ds(0, feats - 1)]),
         (8, g_all.at[pl.ds(0, feats - 1)]), (12, h_all.at[pl.ds(0, feats - 1)]),
     ):
         await_bytes(send_sem.at[phase], ref)
+    if feats > 2:
+        await_bytes(send_sem.at[3], i_all.at[pl.ds(0, feats - 2)])
 
 
 def block_count(rows):
@@ -403,7 +482,7 @@
         pltpu.VMEM((here, 32), BF16),
         pltpu.VMEM((sides, here), F32),
         pltpu.VMEM((sides, here), BF16),
-        pltpu.VMEM((sides, here), F32),
+        pltpu.VMEM((sides, max(here, 2 * width)), F32),
         pltpu.VMEM((sides, LANES), F32),
         pltpu.VMEM((rows, *block), BF16),
         pltpu.VMEM((rows - 1, *block), BF16),

time: 121 us -> 110 us (0.909)
  Pallas kernels: 117 us -> 107 us
    pallas_call x1, Pallas kernels: 117 us -> 107 us  [local(): pl.pallas_call(functools.partial(kernel, sizes), out_shape=(out, out), in...]
where the time goes in v4:
time: 110 us
  Pallas kernels  107 us (97%)
  local copies, waits for them, and re-layouts  2.72 us (2%)
    pallas_call x1, Pallas kernels, local(): pl.pallas_call(functools.partial(kernel, sizes), out_shape=(out, out), in...  107 us
    unnamed x4, local copies, waits for them, and re-layouts  2.72 us

profile of v4, /device:TPU:1, one launch (start us, length us, event | category | flops | bytes accessed | tf_op | source)
XLA Modules:
  0.0 110.3 jit_solution(11780869085908338093)
XLA Ops:
  0.6 107.0 %regress.1 = (f32[32,4096]{1,0:T(8,128)}, f32[32,4096]{1,0:T(8,128)}) custom-call(f32[8,4096]{1,0:T(8,128)} %points.1, s32[8,2048]{1,0:T(8,128)} %freq.1, f32[1,2048]{1,0:T(1,128)} %bitcast.3, f32[1,4096]{1,0:T(1,128)} %bitcast.2, s32[31,4096]{1,0:T(8,128)} %probes.1), custom_call_target="tpu_custom_call" | custom-call | tf_op jit(solution)/shard_map/regress/pallas_call | solution.py:514
  107.6 0.0 copy-start
  107.6 1.9 %copy.9 = f32[32,4096]{1,0:T(8,128)} copy(f32[32,4096]{1,0:T(8,128)} %get-tuple-element.4) | data formatting | bytes 1048576
  109.5 0.0 copy-done
  109.5 0.8 copy.10
Async XLA Ops:
  107.6 1.9 %copy-start = (f32[32,4096]{1,0:T(8,128)S(1)}, f32[32,4096]{1,0:T(8,128)}, u32[]{:S(2)}) copy-start(f32[32,4096]{1,0:T(8,128)} %get-tuple-element.5) | copy-start | bytes 1572868
